TPU v7x, 256 devices: a whole 4x4x8 slice. The times are simulated.
256 devices in a mesh: dp: 32 (over y, z), vocab: 8 (over x, core).
Axes of the slice: x: 4, y: 4, z: 8, core: 2. Of those that a mesh axis runs over, the one named last changes fastest.
Arguments:
- hidden: bfloat16 [24576, 2048], P('dp', 'vocab')
- gain: bfloat16 [2048], replicated, may hold values from 0.5 to 1.5
- head: bfloat16 [2048, 32000], P('dp', 'vocab')
- target_ids: int32 [24576], P('dp'), may hold values from 0 to 31999
- seq_lens: int32 [64], replicated, may hold values from 64 to 704, as said below
- seq_owner: int32 [64], replicated, may hold values from 0 to 31, as said below
Outputs:
- logprob: float32 [24576], P('dp')
- entropy: float32 [24576], P('dp')
Inputs may be any that keep to these rules, and one draw needn't show every extreme that they name: `seq_lens`: the lengths of the sequences owned by one dp index sum to at most 768; in every draw the sequences of some dp index sum to exactly 768. `seq_owner`: every dp index owns exactly 2 sequences.
All inputs are finite; a program needn't handle non-finite values.
Results may differ from a plain program's by a relative error of at most 0.0075.
Values may be sent and summed in bfloat16 or wider, within the bound.
A program may use at most 64 MiB of HBM per device.

v0:
```python
import jax
import jax.numpy as jnp
from jax import lax
from jax.sharding import PartitionSpec as P

EPS = 1e-05


def row_stats(normed, token_ids, columns, offset):
    count = normed.shape[0]
    width = normed.shape[1]
    block_rows = min(128, count)
    blocks = count // block_rows
    breadth = columns.shape[1]

    def compute(block_norm, block_ids):
        logits = jnp.dot(block_norm, columns, preferred_element_type=jnp.float32)
        top = jnp.max(logits, axis=1)
        expo = jnp.exp(logits - top[:, None])
        total = jnp.sum(expo, axis=1)
        weighted = jnp.sum(expo * logits, axis=1)
        local_id = block_ids - offset
        matches = jnp.arange(breadth, dtype=jnp.int32)[None, :] == local_id[:, None]
        picked = jnp.sum(jnp.where(matches, logits, 0.0), axis=1)
        return (top, total, weighted, picked)

    def per_block(item):
        block_norm, block_ids, start = item
        return compute(block_norm, block_ids)

    starts = jnp.arange(blocks, dtype=jnp.int32) * block_rows
    result = lax.map(
        per_block,
        (normed.reshape(blocks, block_rows, width), token_ids.reshape(blocks, block_rows), starts),
    )
    return tuple((member.reshape(count) for member in result))


def local(hidden, gain, head, target_ids, seq_lens, seq_owner):
    groups = lax.axis_size("dp")
    position = lax.axis_index("dp")
    slice_index = lax.axis_index("vocab")
    slots = hidden.shape[0]
    breadth = head.shape[1]
    owners = jnp.arange(groups, dtype=jnp.int32)
    loads = jnp.sum(jnp.where(seq_owner[:, None] == owners[None, :], seq_lens[:, None], 0), axis=0)
    own_live = jnp.arange(slots, dtype=jnp.int32) < loads[position]
    features = lax.all_gather(hidden, "vocab", axis=1, tiled=True)
    wide = features.astype(jnp.float32)
    normed = (
        wide
        * lax.rsqrt(jnp.mean(wide * wide, axis=1, keepdims=True) + EPS)
        * gain.astype(jnp.float32)
    ).astype(jnp.bfloat16)
    columns = lax.all_gather(head, "dp", axis=0, tiled=True)
    stats = row_stats(normed, target_ids, columns, slice_index * breadth)
    top = lax.pmax(stats[0], "vocab")
    factor = jnp.exp(stats[0] - top)
    total, weighted, picked = lax.psum((stats[1] * factor, stats[2] * factor, stats[3]), "vocab")
    lse = top + jnp.log(total)
    logprob = picked - lse
    entropy = lse - weighted / total
    return (jnp.where(own_live, logprob, 0.0), jnp.where(own_live, entropy, 0.0))


def solution(mesh):
    return jax.shard_map(
        local,
        mesh=mesh,
        in_specs=(P("dp", "vocab"), P(), P("dp", "vocab"), P("dp"), P(), P()),
        out_specs=(P("dp"), P("dp")),
        check_vma=False,
    )
```

profile of v0, /device:TPU:8, one launch (start us, length us, event | category | flops | bytes accessed | tf_op | source)
XLA Modules:
  0.0 306.3 jit_solution(14415921997200401669)
XLA Ops:
  7.9 0.7 all-gather.5.cloned.1.call-update
  8.7 0.7 convert_element_type.10
  9.4 0.8 select_reduce_fusion.1
  10.8 36.1 %all-gather.3.cloned.1.call-done = bf16[768,2048]{1,0:T(8,128)(2,1)} async-done(((bf16[768,256]{1,0:T(8,128)(2,1)}), bf16[768,2048]{1,0:T(8,128)(2,1)}) %all-gather.3.cloned.1.call-update) | async-done | bytes 3145744 | tf_op jit(solution)/shard_map/all_gather | solution.py:48
  46.9 2.7 fusion.5
  49.7 2.5 fusion.7
  52.2 137.7 %all-gather.5.cloned.1.call-done = bf16[2048,4000]{1,0:T(8,128)(2,1)} async-done(((bf16[64,4000]{1,0:T(8,128)(2,1)}), bf16[2048,4000]{1,0:T(8,128)(2,1)}) %all-gather.5.cloned.1.call-update) | async-done | bytes 16384016 | tf_op jit(solution)/shard_map/all_gather | solution.py:55
  189.9 70.6 %while.16 = (s32[]{:T(128)}, f32[6,128]{1,0:T(8,128)S(1)}, f32[6,128]{1,0:T(8,128)S(1)}, f32[6,128]{1,0:T(8,128)S(1)}, f32[6,128]{1,0:T(8,128)S(1)}, /*index=5*/...) while((s32[]{:T(128)}, f32[6,128]{1,0:T(8,128)S(1)}, ...), condition=%wide.region_7.8_spmd, body=%wide.region_2.7_spmd.sunk | while | flops 2101247616 | bytes 21406340 | solution.py:32
  189.9 10.2 %fusion.13 = (f32[128]{0:T(128)S(1)}, f32[128,4000]{0,1:T(8,128)S(1)}) fusion(bf16[2048,4000]{1,0:T(8,128)(2,1)} %get-tuple-element.179, bf16[6,128,2048]{2,1,0:T(8,128)(2,1)} %get-tuple-element.178, s32[]{:T(128)} %get-tuple-element.162), kind=kOutput, calls=%fused_computation.25.clone.1 | convolution fusion | flops 2097663872 | bytes 19350528 | tf_op jit(solution)/shard_map/while/body/eval_jaxpr/dot_general | solution.py:17
  200.1 0.7 subtract_bitcast_fusion.2
  201.6 10.2 %fusion.13 = (f32[128]{0:T(128)S(1)}, f32[128,4000]{0,1:T(8,128)S(1)}) fusion(bf16[2048,4000]{1,0:T(8,128)(2,1)} %get-tuple-element.179, bf16[6,128,2048]{2,1,0:T(8,128)(2,1)} %get-tuple-element.178, s32[]{:T(128)} %get-tuple-element.162), kind=kOutput, calls=%fused_computation.25.clone.1 | convolution fusion | flops 2097663872 | bytes 19350528 | tf_op jit(solution)/shard_map/while/body/eval_jaxpr/dot_general | solution.py:17
  211.9 0.7 subtract_bitcast_fusion.2
  213.4 10.2 %fusion.13 = (f32[128]{0:T(128)S(1)}, f32[128,4000]{0,1:T(8,128)S(1)}) fusion(bf16[2048,4000]{1,0:T(8,128)(2,1)} %get-tuple-element.179, bf16[6,128,2048]{2,1,0:T(8,128)(2,1)} %get-tuple-element.178, s32[]{:T(128)} %get-tuple-element.162), kind=kOutput, calls=%fused_computation.25.clone.1 | convolution fusion | flops 2097663872 | bytes 19350528 | tf_op jit(solution)/shard_map/while/body/eval_jaxpr/dot_general | solution.py:17
  223.7 0.7 subtract_bitcast_fusion.2
  225.2 10.2 %fusion.13 = (f32[128]{0:T(128)S(1)}, f32[128,4000]{0,1:T(8,128)S(1)}) fusion(bf16[2048,4000]{1,0:T(8,128)(2,1)} %get-tuple-element.179, bf16[6,128,2048]{2,1,0:T(8,128)(2,1)} %get-tuple-element.178, s32[]{:T(128)} %get-tuple-element.162), kind=kOutput, calls=%fused_computation.25.clone.1 | convolution fusion | flops 2097663872 | bytes 19350528 | tf_op jit(solution)/shard_map/while/body/eval_jaxpr/dot_general | solution.py:17
  235.4 0.7 subtract_bitcast_fusion.2
  236.1 0.7 multiply_reduce_fusion.2
  237.0 10.2 %fusion.13 = (f32[128]{0:T(128)S(1)}, f32[128,4000]{0,1:T(8,128)S(1)}) fusion(bf16[2048,4000]{1,0:T(8,128)(2,1)} %get-tuple-element.179, bf16[6,128,2048]{2,1,0:T(8,128)(2,1)} %get-tuple-element.178, s32[]{:T(128)} %get-tuple-element.162), kind=kOutput, calls=%fused_computation.25.clone.1 | convolution fusion | flops 2097663872 | bytes 19350528 | tf_op jit(solution)/shard_map/while/body/eval_jaxpr/dot_general | solution.py:17
  247.2 0.7 subtract_bitcast_fusion.2
  248.7 10.2 %fusion.13 = (f32[128]{0:T(128)S(1)}, f32[128,4000]{0,1:T(8,128)S(1)}) fusion(bf16[2048,4000]{1,0:T(8,128)(2,1)} %get-tuple-element.179, bf16[6,128,2048]{2,1,0:T(8,128)(2,1)} %get-tuple-element.178, s32[]{:T(128)} %get-tuple-element.162), kind=kOutput, calls=%fused_computation.25.clone.1 | convolution fusion | flops 2097663872 | bytes 19350528 | tf_op jit(solution)/shard_map/while/body/eval_jaxpr/dot_general | solution.py:17
  259.0 0.7 subtract_bitcast_fusion.2
  260.5 14.1 %pmax.7 = f32[768]{0:T(1024)S(1)} all-reduce(f32[768]{0:T(1024)S(1)} %bitcast.42), channel_id=1, replica_groups=mesh['dp'=32,'vocab'=8] {'vocab'}, use_global_device_ids=true, to_apply=%region_9.10 | all-reduce | flops 768 | bytes 6144 | tf_op jit(solution)/shard_map/pmax | solution.py:57
  274.7 23.6 %all-reduce = (f32[768]{0:T(1024)S(1)}, f32[768]{0:T(1024)S(1)}, f32[768]{0:T(1024)S(1)}) all-reduce(f32[768]{0:T(1024)S(1)} %bitcast.43, f32[768]{0:T(1024)S(1)} %get-tuple-element.85, f32[768]{0:T(1024)S(1)} %get-tuple-element.84), channel_id=1, replica_groups=mesh['dp'=32,'vocab'=8] {'vocab'}, use_global_device_ids=true, to_apply=%region_8.9 | all-reduce | flops 2304 | bytes 18432 | tf_op jit(solution)/shard_map/psum | solution.py:59
  298.2 1.2 subtract_select_fusion
  (41 shorter events, 5.7 us)
Async XLA Ops:
  7.2 39.7 %all-gather.3.cloned.1.call-start = ((), (), s32[]{:S(2)}) async-start(), calls=%async_computation | async-start | bytes 3538944 | tf_op jit(solution)/shard_map/all_gather | solution.py:48
  7.9 182.0 %all-gather.5.cloned.1.call-start = ((), (), s32[]{:S(2)}) async-start(), calls=%async_computation.1 | async-start | bytes 17301504 | tf_op jit(solution)/shard_map/all_gather | solution.py:55
  46.9 2.8 copy-start
Sparse Core Ops, SparseCore 0:
  9.8 37.0 all-gather.2
  49.5 140.3 all-gather.4
where the time goes:
time: 307 us; the launch traced here: 306 us
  waiting for transfers between devices  175 us (57%)
  matrix products  61.4 us (20%)
  blocking collectives  37.7 us (12%)
  other arithmetic  16.2 us (5%)
  between operations  14.1 us (5%)
    all_gather x1, waiting for transfers between devices, local(): columns = lax.all_gather(head, 'dp', axis=0, tiled=True)  138 us
    dot_general x6, matrix products, compute(): logits = jnp.dot(block_norm, columns, preferred_element_type=jnp.float32)  61.4 us
    all_gather x1, waiting for transfers between devices, local(): features = lax.all_gather(hidden, 'vocab', axis=1, tiled=True)  36.1 us
    psum x1, blocking collectives, local(): lax.psum((stats[1] * factor, stats[2] * factor, stats[3]), 'vocab')  23.6 us
    pmax x1, blocking collectives, local(): top = lax.pmax(stats[0], 'vocab')  14.1 us
  transfers between devices with their start and end apart: 2, of which 2 were waited for; matrix products, arithmetic and copies ran while one was open for 2% of the time, Pallas kernels for 0%

commit v1 on v0

--- a/solution.py
+++ b/solution.py
@@ -45,7 +45,9 @@
     owners = jnp.arange(groups, dtype=jnp.int32)
     loads = jnp.sum(jnp.where(seq_owner[:, None] == owners[None, :], seq_lens[:, None], 0), axis=0)
     own_live = jnp.arange(slots, dtype=jnp.int32) < loads[position]
-    features = lax.all_gather(hidden, "vocab", axis=1, tiled=True)
+    features = jnp.concatenate(
+        lax.all_to_all(jnp.stack([hidden] * lax.axis_size("vocab")), "vocab", 0, 0), axis=1
+    )
     wide = features.astype(jnp.float32)
     normed = (
         wide

time: 307 us -> 270 us (0.88)
  waiting for transfers between devices: 175 us -> 117 us
  local copies, waits for them, and re-layouts: 1.51 us -> 17.7 us
  starting transfers between devices: 0.08 us -> 4.47 us
    all_gather x1, waiting for transfers between devices: 138 us -> 79.2 us  [local(): columns = lax.all_gather(head, 'dp', axis=0, tiled=True)]
    all_to_all x0 -> x1, waiting for transfers between devices: none -> 37.6 us  [local(): lax.all_to_all(jnp.stack([hidden] * lax.axis_size('vocab')), 'vocab', 0, 0)]
    all_gather x1 -> x0, waiting for transfers between devices: 36.1 us -> none  [local(): features = lax.all_gather(hidden, 'vocab', axis=1, tiled=True)]
    convert_element_type x0 -> x2, local copies, waits for them, and re-layouts: none -> 13.4 us  [local(): wide = features.astype(jnp.float32)]
    all_to_all x0 -> x1, starting transfers between devices: none -> 4.43 us  [local(): lax.all_to_all(jnp.stack([hidden] * lax.axis_size('vocab')), 'vocab', 0, 0)]
  transfers between devices with their start and end apart: 2 -> 2, of which waited for: 2 -> 2; matrix products, arithmetic and copies ran while one was open for 2% -> 9% of each run, Pallas kernels for 0% -> 0%
where the time goes in v1:
time: 270 us; the launch traced here: 269 us
  waiting for transfers between devices  117 us (43%)
  matrix products  61.4 us (23%)
  blocking collectives  37.7 us (14%)
  local copies, waits for them, and re-layouts  17.7 us (7%)
  other arithmetic  16.2 us (6%)
  between operations  14.1 us (5%)
  starting transfers between devices  4.47 us (2%)
    all_gather x1, waiting for transfers between devices, local(): columns = lax.all_gather(head, 'dp', axis=0, tiled=True)  79.2 us
    dot_general x6, matrix products, compute(): logits = jnp.dot(block_norm, columns, preferred_element_type=jnp.float32)  61.4 us
    all_to_all x1, waiting for transfers between devices, local(): lax.all_to_all(jnp.stack([hidden] * lax.axis_size('vocab')), 'vocab', 0, 0)  37.6 us
    psum x1, blocking collectives, local(): lax.psum((stats[1] * factor, stats[2] * factor, stats[3]), 'vocab')  23.6 us
    pmax x1, blocking collectives, local(): top = lax.pmax(stats[0], 'vocab')  14.1 us
    convert_element_type x2, local copies, waits for them, and re-layouts, local(): wide = features.astype(jnp.float32)  13.4 us
  transfers between devices with their start and end apart: 2, of which 2 were waited for; matrix products, arithmetic and copies ran while one was open for 9% of the time, Pallas kernels for 0%

profile of v1, /device:TPU:8, one launch (start us, length us, event | category | flops | bytes accessed | tf_op | source)
XLA Modules:
  0.0 269.3 jit_solution(14433939102058908429)
XLA Ops:
  7.9 2.9 %stack.2 = bf16[8,768,256]{2,1,0:T(8,128)(2,1)} broadcast(bf16[768,256]{1,0:T(8,128)(2,1)} %param.8), dimensions={1,2} | broadcast | bytes 3538944 | tf_op jit(solution)/shard_map/stack | solution.py:49
  10.8 4.4 %all-to-all-start = ((bf16[8,768,256]{2,1,0:T(8,128)(2,1)}), bf16[8,768,256]{2,1,0:T(8,128)(2,1)S(1)}, u32[]{:S(2)}, u32[]{:S(2)}) async-start(bf16[8,768,256]{2,1,0:T(8,128)(2,1)} %stack.2), calls=%async_computation | async-start | bytes 6291456 | tf_op jit(solution)/shard_map/all_to_all | solution.py:49
  16.0 37.6 %all-to-all-done = bf16[8,768,256]{2,1,0:T(8,128)(2,1)S(1)} async-done(((bf16[8,768,256]{2,1,0:T(8,128)(2,1)}), bf16[8,768,256]{2,1,0:T(8,128)(2,1)S(1)}, u32[]{:S(2)}, u32[]{:S(2)}) %all-to-all-start) | async-done | bytes 3145760 | tf_op jit(solution)/shard_map/all_to_all | solution.py:49
  54.2 6.3 %copy.9 = f32[768,8,256]{2,1,0:T(8,128)} copy(f32[768,8,256]{2,0,1:T(8,128)S(1)} %convert_bitcast_fusion) | data formatting | bytes 12582912 | tf_op jit(solution)/shard_map/convert_element_type | solution.py:51
  60.5 7.1 %reshape.67 = f32[6,128,2048]{2,1,0:T(8,128)} reshape(f32[768,8,256]{2,1,0:T(8,128)} %copy.9) | data formatting | bytes 12582912 | tf_op jit(solution)/shard_map/convert_element_type | solution.py:51
  67.6 0.7 fusion.5
  68.3 5.3 %multiply_convert_fusion = bf16[6,128,2048]{2,1,0:T(8,128)(2,1)} fusion(f32[6,128,2048]{2,1,0:T(8,128)} %reshape.67, f32[2048]{0:T(1024)S(1)} %convert_element_type.25, f32[6,128]{1,0:T(8,128)S(1)} %rsqrt_bitcast_fusion), kind=kLoop, calls=%fused_computation.13 | loop fusion | flops 4718592 | bytes 9448448 | tf_op jit(solution)/shard_map/convert_element_type | solution.py:56
  73.6 79.2 %all-gather.2.cloned.1.call-done = bf16[2048,4000]{1,0:T(8,128)(2,1)} async-done(((bf16[64,4000]{1,0:T(8,128)(2,1)}), bf16[2048,4000]{1,0:T(8,128)(2,1)}) %all-gather.2.cloned.1.call-update) | async-done | bytes 16384016 | tf_op jit(solution)/shard_map/all_gather | solution.py:57
  152.8 70.6 %while.16 = (s32[]{:T(128)}, f32[6,128]{1,0:T(8,128)S(1)}, f32[6,128]{1,0:T(8,128)S(1)}, f32[6,128]{1,0:T(8,128)S(1)}, f32[6,128]{1,0:T(8,128)S(1)}, /*index=5*/...) while((s32[]{:T(128)}, f32[6,128]{1,0:T(8,128)S(1)}, ...), condition=%wide.region_7.8_spmd, body=%wide.region_2.7_spmd.sunk | while | flops 2101247616 | bytes 21406340 | solution.py:32
  152.8 10.2 %fusion.11 = (f32[128]{0:T(128)S(1)}, f32[128,4000]{0,1:T(8,128)S(1)}) fusion(bf16[2048,4000]{1,0:T(8,128)(2,1)} %get-tuple-element.179, bf16[6,128,2048]{2,1,0:T(8,128)(2,1)} %get-tuple-element.178, s32[]{:T(128)} %get-tuple-element.162), kind=kOutput, calls=%fused_computation.24.clone.1 | convolution fusion | flops 2097663872 | bytes 19350528 | tf_op jit(solution)/shard_map/while/body/eval_jaxpr/dot_general | solution.py:17
  163.0 0.7 subtract_bitcast_fusion.2
  164.6 10.2 %fusion.11 = (f32[128]{0:T(128)S(1)}, f32[128,4000]{0,1:T(8,128)S(1)}) fusion(bf16[2048,4000]{1,0:T(8,128)(2,1)} %get-tuple-element.179, bf16[6,128,2048]{2,1,0:T(8,128)(2,1)} %get-tuple-element.178, s32[]{:T(128)} %get-tuple-element.162), kind=kOutput, calls=%fused_computation.24.clone.1 | convolution fusion | flops 2097663872 | bytes 19350528 | tf_op jit(solution)/shard_map/while/body/eval_jaxpr/dot_general | solution.py:17
  174.8 0.7 subtract_bitcast_fusion.2
  176.4 10.2 %fusion.11 = (f32[128]{0:T(128)S(1)}, f32[128,4000]{0,1:T(8,128)S(1)}) fusion(bf16[2048,4000]{1,0:T(8,128)(2,1)} %get-tuple-element.179, bf16[6,128,2048]{2,1,0:T(8,128)(2,1)} %get-tuple-element.178, s32[]{:T(128)} %get-tuple-element.162), kind=kOutput, calls=%fused_computation.24.clone.1 | convolution fusion | flops 2097663872 | bytes 19350528 | tf_op jit(solution)/shard_map/while/body/eval_jaxpr/dot_general | solution.py:17
  186.6 0.7 subtract_bitcast_fusion.2
  188.1 10.2 %fusion.11 = (f32[128]{0:T(128)S(1)}, f32[128,4000]{0,1:T(8,128)S(1)}) fusion(bf16[2048,4000]{1,0:T(8,128)(2,1)} %get-tuple-element.179, bf16[6,128,2048]{2,1,0:T(8,128)(2,1)} %get-tuple-element.178, s32[]{:T(128)} %get-tuple-element.162), kind=kOutput, calls=%fused_computation.24.clone.1 | convolution fusion | flops 2097663872 | bytes 19350528 | tf_op jit(solution)/shard_map/while/body/eval_jaxpr/dot_general | solution.py:17
  198.4 0.7 subtract_bitcast_fusion.2
  199.9 10.2 %fusion.11 = (f32[128]{0:T(128)S(1)}, f32[128,4000]{0,1:T(8,128)S(1)}) fusion(bf16[2048,4000]{1,0:T(8,128)(2,1)} %get-tuple-element.179, bf16[6,128,2048]{2,1,0:T(8,128)(2,1)} %get-tuple-element.178, s32[]{:T(128)} %get-tuple-element.162), kind=kOutput, calls=%fused_computation.24.clone.1 | convolution fusion | flops 2097663872 | bytes 19350528 | tf_op jit(solution)/shard_map/while/body/eval_jaxpr/dot_general | solution.py:17
  210.2 0.7 subtract_bitcast_fusion.2
  211.7 10.2 %fusion.11 = (f32[128]{0:T(128)S(1)}, f32[128,4000]{0,1:T(8,128)S(1)}) fusion(bf16[2048,4000]{1,0:T(8,128)(2,1)} %get-tuple-element.179, bf16[6,128,2048]{2,1,0:T(8,128)(2,1)} %get-tuple-element.178, s32[]{:T(128)} %get-tuple-element.162), kind=kOutput, calls=%fused_computation.24.clone.1 | convolution fusion | flops 2097663872 | bytes 19350528 | tf_op jit(solution)/shard_map/while/body/eval_jaxpr/dot_general | solution.py:17
  221.9 0.7 subtract_bitcast_fusion.2
  223.5 14.1 %pmax.7 = f32[768]{0:T(1024)S(1)} all-reduce(f32[768]{0:T(1024)S(1)} %bitcast.44), channel_id=1, replica_groups=mesh['dp'=32,'vocab'=8] {'vocab'}, use_global_device_ids=true, to_apply=%region_9.10 | all-reduce | flops 768 | bytes 6144 | tf_op jit(solution)/shard_map/pmax | solution.py:59
  237.6 23.6 %all-reduce = (f32[768]{0:T(1024)S(1)}, f32[768]{0:T(1024)S(1)}, f32[768]{0:T(1024)S(1)}) all-reduce(f32[768]{0:T(1024)S(1)} %bitcast.45, f32[768]{0:T(1024)S(1)} %get-tuple-element.85, f32[768]{0:T(1024)S(1)} %get-tuple-element.84), channel_id=1, replica_groups=mesh['dp'=32,'vocab'=8] {'vocab'}, use_global_device_ids=true, to_apply=%region_8.9 | all-reduce | flops 2304 | bytes 18432 | tf_op jit(solution)/shard_map/psum | solution.py:61
  261.2 1.3 subtract_select_fusion
  (48 shorter events, 7.0 us)
Async XLA Ops:
  7.2 145.7 %all-gather.2.cloned.1.call-start = ((), (), s32[]{:S(2)}) async-start(), calls=%async_computation.1 | async-start | bytes 17301504 | tf_op jit(solution)/shard_map/all_gather | solution.py:57
  10.8 4.5 %copy-start = (bf16[2048]{0:T(1024)(128)(2,1)S(1)}, bf16[2048]{0:T(1024)(128)(2,1)}, u32[]{:S(2)}) copy-start(bf16[2048]{0:T(1024)(128)(2,1)} %param.9) | copy-start | bytes 12292
  10.8 4.5 %copy-start.1 = (s32[64]{0:T(128)S(1)}, s32[64]{0:T(128)}, u32[]{:S(2)}) copy-start(s32[64]{0:T(128)} %param.12) | copy-start | bytes 772
  10.8 4.5 %copy-start.2 = (s32[64]{0:T(128)S(1)}, s32[64]{0:T(128)}, u32[]{:S(2)}) copy-start(s32[64]{0:T(128)} %param.13) | copy-start | bytes 772
  10.8 42.9 %all-to-all-start = ((bf16[8,768,256]{2,1,0:T(8,128)(2,1)}), bf16[8,768,256]{2,1,0:T(8,128)(2,1)S(1)}, u32[]{:S(2)}, u32[]{:S(2)}) async-start(bf16[8,768,256]{2,1,0:T(8,128)(2,1)} %stack.2), calls=%async_computation | async-start | bytes 6291456 | tf_op jit(solution)/shard_map/all_to_all | solution.py:49
Sparse Core Ops, SparseCore 0:
  10.6 142.1 all-gather.1
